TPU v7x, 32 devices: a whole 2x2x4 slice. The times are simulated.
32 devices in a mesh: expert: 4 (over z), fsdp: 8 (over y, x, core).
Axes of the slice: x: 2, y: 2, z: 4, core: 2. Of those that a mesh axis runs over, the one named last changes fastest.
Arguments:
- tokens: bfloat16 [25216, 512], P(('expert', 'fsdp')), may hold values from -6 to 6
- routes: int32 [25216, 2], P(('expert', 'fsdp')), may hold values from 0 to 7, all different within a row; in each aligned block of 788 rows (0 to 787, 788 to 1575, ...) at most 394 rows name the same one
- cotangent: bfloat16 [25216, 512], P(('expert', 'fsdp')), may hold values from -6 to 6
- attend_gain: float32 [512], P('fsdp'), may hold values from 0.5 to 1.5
- attend_bias: float32 [512], P('fsdp'), may hold values from -1.25 to 1.25
- triple_weight: float32 [512, 1536], P('fsdp'), may hold values from -0.25 to 0.25
- merge_weight: float32 [512, 512], P('fsdp'), may hold values from -2 to 2
- mixture_gain: float32 [512], P('fsdp'), may hold values from 0.5 to 1.5
- mixture_bias: float32 [512], P('fsdp'), may hold values from -1.25 to 1.25
- router_weight: float32 [512, 8], P('fsdp'), may hold values from -0.125 to 0.125
- expert_up: float32 [8, 512, 2048], P('expert', 'fsdp'), may hold values from -0.25 to 0.25
- expert_down: float32 [8, 2048, 512], P('expert', 'fsdp'), may hold values from -0.75 to 0.75
Outputs:
- block_out: bfloat16 [25216, 512], P(('expert', 'fsdp'))
- tokens_grad: float32 [25216, 512], P(('expert', 'fsdp'))
- attendgain_grad: float32 [512], P('fsdp')
- attendbias_grad: float32 [512], P('fsdp')
- triple_grad: float32 [512, 1536], P('fsdp')
- merge_grad: float32 [512, 512], P('fsdp')
- mixturegain_grad: float32 [512], P('fsdp')
- mixturebias_grad: float32 [512], P('fsdp')
- router_grad: float32 [512, 8], P('fsdp')
- expertup_grad: float32 [8, 512, 2048], P('expert', 'fsdp')
- expertdown_grad: float32 [8, 2048, 512], P('expert', 'fsdp')
Inputs may be any that keep to these rules, and one draw needn't show every extreme that they name: `routes`: each token names 2 different experts. Among the 788 tokens of one device no expert is named by more than 394 tokens, a bound that some block reaches of them; every expert is named by some token.
All inputs are finite; a program needn't handle non-finite values.
Results may differ from a plain program's by a relative error of at most 0.02.
Values may be sent and summed in bfloat16 or wider, within the bound.
A program may use at most 192 MiB of HBM per device.

v0:
```python
from functools import partial
import jax
import jax.numpy as jnp
from jax import lax
from jax.sharding import PartitionSpec as P

HEAD_DIM = 64
TOP = 2
SEQ = 197
EPSILON = 1e-06


def layer_norm(values, gain, bias):
    center = values - jnp.mean(values, -1, keepdims=True)
    spread = jnp.mean(center * center, -1, keepdims=True)
    return center * lax.rsqrt(spread + EPSILON) * gain + bias


def local(
    tokens,
    routes,
    cotangent,
    attend_gain,
    attend_bias,
    triple_weight,
    merge_weight,
    mixture_gain,
    mixture_bias,
    router_weight,
    expert_up,
    expert_down,
):
    local_rows = tokens.shape[0]
    width = tokens.shape[1]
    experts = router_weight.shape[1]
    owners = lax.axis_size("expert")
    per_owner = expert_up.shape[0]
    capacity = 2 * TOP * local_rows // experts
    images = local_rows // SEQ
    heads = width // HEAD_DIM
    scale = 1.0 / HEAD_DIM**0.5
    spread_rows = owners * capacity
    gain_one, bias_one, triple, merge_full, gain_two, bias_two, router = (
        lax.all_gather(attend_gain.astype(jnp.bfloat16), "fsdp", axis=0, tiled=True),
        lax.all_gather(attend_bias.astype(jnp.bfloat16), "fsdp", axis=0, tiled=True),
        lax.all_gather(triple_weight.astype(jnp.bfloat16), "fsdp", axis=0, tiled=True),
        lax.all_gather(merge_weight.astype(jnp.bfloat16), "fsdp", axis=0, tiled=True),
        lax.all_gather(mixture_gain.astype(jnp.bfloat16), "fsdp", axis=0, tiled=True),
        lax.all_gather(mixture_bias.astype(jnp.bfloat16), "fsdp", axis=0, tiled=True),
        lax.all_gather(router_weight.astype(jnp.bfloat16), "fsdp", axis=0, tiled=True),
    )
    up_full, down_full = (
        lax.all_gather(expert_up.astype(jnp.bfloat16), "fsdp", axis=1, tiled=True),
        lax.all_gather(expert_down.astype(jnp.bfloat16), "fsdp", axis=1, tiled=True),
    )
    inputs = tokens.astype(jnp.float32)
    normed_one, norm_back_one = jax.vjp(
        layer_norm, inputs, gain_one.astype(jnp.float32), bias_one.astype(jnp.float32)
    )
    normed_low = normed_one.astype(jnp.bfloat16)
    joined = jnp.dot(normed_low, triple, preferred_element_type=jnp.float32).astype(jnp.bfloat16)
    joined = joined.reshape(images, SEQ, 3, heads, HEAD_DIM)
    query_rows = joined[:, :, 0]
    key_rows = joined[:, :, 1]
    value_rows = joined[:, :, 2]
    scores = (
        jnp.einsum("bqhd,bkhd->bhqk", query_rows, key_rows, preferred_element_type=jnp.float32)
        * scale
    )
    top_score = jnp.max(scores, -1, keepdims=True)
    log_total = top_score + jnp.log(jnp.sum(jnp.exp(scores - top_score), -1, keepdims=True))
    weights_low = jnp.exp(scores - log_total).astype(jnp.bfloat16)
    mixed = jnp.einsum(
        "bhqk,bkhd->bqhd", weights_low, value_rows, preferred_element_type=jnp.float32
    )
    mixed = mixed.astype(jnp.bfloat16).reshape(local_rows, width)
    branch = jnp.dot(mixed, merge_full, preferred_element_type=jnp.float32)
    hidden_one = inputs + branch
    normed_two, norm_back_two = jax.vjp(
        layer_norm, hidden_one, gain_two.astype(jnp.float32), bias_two.astype(jnp.float32)
    )
    send_rows = normed_two.astype(jnp.bfloat16)
    logits = jnp.dot(send_rows, router, preferred_element_type=jnp.float32)
    probs = jax.nn.softmax(logits, -1)
    expert_ids = jnp.arange(experts, dtype=jnp.int32)
    picked = (routes[:, :, None] == expert_ids).astype(jnp.float32)
    gates = jnp.sum(picked * probs[:, None, :], 2)
    chosen = routes.reshape(-1)
    onehot = (chosen[:, None] == expert_ids).astype(jnp.int32)
    before = jnp.cumsum(onehot, 0) - onehot
    ranking = jnp.sum(before * onehot, 1)
    slots = chosen * capacity + ranking
    pair_ids = jnp.arange(chosen.shape[0], dtype=jnp.int32)
    filler = jnp.zeros((experts * capacity,), jnp.int32).at[slots].set(pair_ids + 1)
    token_source = jnp.where(filler > 0, (filler - 1) // TOP + 1, 0)
    padded = jnp.concatenate([jnp.zeros((1, width), jnp.bfloat16), send_rows], 0)
    outgoing = padded[token_source].reshape(owners, per_owner, capacity, width)
    arrived = lax.all_to_all(outgoing, "expert", split_axis=0, concat_axis=2, tiled=True).reshape(
        per_owner, spread_rows, width
    )
    hidden_list = []
    active_list = []
    result_list = []
    for member in range(per_owner):
        hidden_pre = jnp.dot(arrived[member], up_full[member], preferred_element_type=jnp.float32)
        activated = jax.nn.gelu(hidden_pre, approximate=False).astype(jnp.bfloat16)
        hidden_list.append(hidden_pre)
        active_list.append(activated)
        result_list.append(
            jnp.dot(activated, down_full[member], preferred_element_type=jnp.float32).astype(
                jnp.bfloat16
            )
        )
    expert_out = jnp.stack(result_list, 0).reshape(1, per_owner, spread_rows, width)
    returned = lax.all_to_all(expert_out, "expert", split_axis=2, concat_axis=0, tiled=True)
    pair_out = (
        returned.reshape(experts * capacity, width)[slots]
        .reshape(local_rows, TOP, width)
        .astype(jnp.float32)
    )
    mixture = jnp.sum(gates[:, :, None] * pair_out, 1)
    block_out = (hidden_one + mixture).astype(jnp.bfloat16)
    upstream = cotangent.astype(jnp.float32)
    gate_grad = jnp.sum(upstream[:, None, :] * pair_out, 2)
    pair_grad = (
        (gates[:, :, None] * upstream[:, None, :])
        .astype(jnp.bfloat16)
        .reshape(local_rows * TOP, width)
    )
    padded_grad = jnp.concatenate([jnp.zeros((1, width), jnp.bfloat16), pair_grad], 0)
    outgoing_grad = padded_grad[filler].reshape(owners, per_owner, capacity, width)
    arrived_grad = lax.all_to_all(
        outgoing_grad, "expert", split_axis=0, concat_axis=2, tiled=True
    ).reshape(per_owner, spread_rows, width)
    up_back, down_back = (
        lax.all_gather(expert_up.astype(jnp.bfloat16), "fsdp", axis=1, tiled=True),
        lax.all_gather(expert_down.astype(jnp.bfloat16), "fsdp", axis=1, tiled=True),
    )
    up_list = []
    down_list = []
    row_list = []
    for member in range(per_owner):
        act_grad = jnp.dot(
            arrived_grad[member], down_back[member].T, preferred_element_type=jnp.float32
        )
        down_list.append(
            jnp.dot(active_list[member].T, arrived_grad[member], preferred_element_type=jnp.float32)
        )
        gelu_back = jax.vjp(partial(jax.nn.gelu, approximate=False), hidden_list[member])[1]
        pre_grad = gelu_back(act_grad)[0].astype(jnp.bfloat16)
        up_list.append(jnp.dot(arrived[member].T, pre_grad, preferred_element_type=jnp.float32))
        row_list.append(
            jnp.dot(pre_grad, up_back[member].T, preferred_element_type=jnp.float32).astype(
                jnp.bfloat16
            )
        )
    row_grad = jnp.stack(row_list, 0).reshape(1, per_owner, spread_rows, width)
    back_rows = lax.all_to_all(row_grad, "expert", split_axis=2, concat_axis=0, tiled=True)
    send_grad = jnp.sum(
        back_rows.reshape(experts * capacity, width)[slots]
        .reshape(local_rows, TOP, width)
        .astype(jnp.float32),
        1,
    )
    up_total = jnp.stack(up_list, 0)
    down_total = jnp.stack(down_list, 0)
    expertup_grad, expertdown_grad = (
        lax.psum_scatter(
            up_total.astype(jnp.bfloat16), "fsdp", scatter_dimension=1, tiled=True
        ).astype(jnp.float32),
        lax.psum_scatter(
            down_total.astype(jnp.bfloat16), "fsdp", scatter_dimension=1, tiled=True
        ).astype(jnp.float32),
    )
    prob_grad = jnp.sum(picked * gate_grad[:, :, None], 1)
    logit_grad = (probs * (prob_grad - jnp.sum(probs * prob_grad, -1, keepdims=True))).astype(
        jnp.bfloat16
    )
    router_term = jnp.dot(send_rows.T, logit_grad, preferred_element_type=jnp.float32)
    normed_grad = send_grad + jnp.dot(logit_grad, router.T, preferred_element_type=jnp.float32)
    hidden_grad, gain_two_term, bias_two_term = norm_back_two(normed_grad)
    hidden_grad = hidden_grad + upstream
    branch_grad = hidden_grad.astype(jnp.bfloat16)
    merge_term = jnp.dot(mixed.T, branch_grad, preferred_element_type=jnp.float32)
    mixed_grad = jnp.dot(branch_grad, merge_full.T, preferred_element_type=jnp.float32).astype(
        jnp.bfloat16
    )
    mixed_grad = mixed_grad.reshape(images, SEQ, heads, HEAD_DIM)
    scores_again = (
        jnp.einsum("bqhd,bkhd->bhqk", query_rows, key_rows, preferred_element_type=jnp.float32)
        * scale
    )
    probs_again = jnp.exp(scores_again - log_total)
    weight_grad = jnp.einsum(
        "bqhd,bkhd->bhqk", mixed_grad, value_rows, preferred_element_type=jnp.float32
    )
    score_grad = (
        probs_again * (weight_grad - jnp.sum(probs_again * weight_grad, -1, keepdims=True))
    ).astype(jnp.bfloat16)
    query_grad = (
        jnp.einsum("bhqk,bkhd->bqhd", score_grad, key_rows, preferred_element_type=jnp.float32)
        * scale
    )
    key_grad = (
        jnp.einsum("bhqk,bqhd->bkhd", score_grad, query_rows, preferred_element_type=jnp.float32)
        * scale
    )
    value_grad = jnp.einsum(
        "bhqk,bqhd->bkhd",
        probs_again.astype(jnp.bfloat16),
        mixed_grad,
        preferred_element_type=jnp.float32,
    )
    joined_grad = (
        jnp.stack([query_grad, key_grad, value_grad], 2)
        .astype(jnp.bfloat16)
        .reshape(local_rows, 3 * width)
    )
    triple_term = jnp.dot(normed_low.T, joined_grad, preferred_element_type=jnp.float32)
    normed_one_grad = jnp.dot(joined_grad, triple.T, preferred_element_type=jnp.float32)
    input_grad, gain_one_term, bias_one_term = norm_back_one(normed_one_grad)
    tokens_grad = input_grad + hidden_grad
    shares = (
        lax.psum_scatter(
            gain_one_term.astype(jnp.bfloat16), "fsdp", scatter_dimension=0, tiled=True
        ).astype(jnp.float32),
        lax.psum_scatter(
            bias_one_term.astype(jnp.bfloat16), "fsdp", scatter_dimension=0, tiled=True
        ).astype(jnp.float32),
        lax.psum_scatter(
            triple_term.astype(jnp.bfloat16), "fsdp", scatter_dimension=0, tiled=True
        ).astype(jnp.float32),
        lax.psum_scatter(
            merge_term.astype(jnp.bfloat16), "fsdp", scatter_dimension=0, tiled=True
        ).astype(jnp.float32),
        lax.psum_scatter(
            gain_two_term.astype(jnp.bfloat16), "fsdp", scatter_dimension=0, tiled=True
        ).astype(jnp.float32),
        lax.psum_scatter(
            bias_two_term.astype(jnp.bfloat16), "fsdp", scatter_dimension=0, tiled=True
        ).astype(jnp.float32),
        lax.psum_scatter(
            router_term.astype(jnp.bfloat16), "fsdp", scatter_dimension=0, tiled=True
        ).astype(jnp.float32),
    )
    totals = (
        lax.psum(shares[0].astype(jnp.bfloat16), "expert").astype(jnp.float32),
        lax.psum(shares[1].astype(jnp.bfloat16), "expert").astype(jnp.float32),
        lax.psum(shares[2].astype(jnp.bfloat16), "expert").astype(jnp.float32),
        lax.psum(shares[3].astype(jnp.bfloat16), "expert").astype(jnp.float32),
        lax.psum(shares[4].astype(jnp.bfloat16), "expert").astype(jnp.float32),
        lax.psum(shares[5].astype(jnp.bfloat16), "expert").astype(jnp.float32),
        lax.psum(shares[6].astype(jnp.bfloat16), "expert").astype(jnp.float32),
    )
    return (
        block_out,
        tokens_grad,
        totals[0],
        totals[1],
        totals[2],
        totals[3],
        totals[4],
        totals[5],
        totals[6],
        expertup_grad,
        expertdown_grad,
    )


def solution(mesh):
    return jax.shard_map(
        local,
        mesh=mesh,
        in_specs=(
            P(("expert", "fsdp"), None),
            P(("expert", "fsdp"), None),
            P(("expert", "fsdp"), None),
            P("fsdp"),
            P("fsdp"),
            P("fsdp", None),
            P("fsdp", None),
            P("fsdp"),
            P("fsdp"),
            P("fsdp", None),
            P("expert", "fsdp", None),
            P("expert", "fsdp", None),
        ),
        out_specs=(
            P(("expert", "fsdp"), None),
            P(("expert", "fsdp"), None),
            P("fsdp"),
            P("fsdp"),
            P("fsdp", None),
            P("fsdp", None),
            P("fsdp"),
            P("fsdp"),
            P("fsdp", None),
            P("expert", "fsdp", None),
            P("expert", "fsdp", None),
        ),
        check_vma=False,
    )
```

profile of v0, /device:TPU:0, one launch (start us, length us, event | category | flops | bytes accessed | tf_op | source)
XLA Modules:
  0.0 934.5 jit_solution(5010760115874107428)
XLA Ops:
  15.2 15.2 %all-reduce.12 = (bf16[512]{0:T(512)(128)(2,1)S(1)}, bf16[512]{0:T(512)(128)(2,1)S(1)}, bf16[512]{0:T(512)(128)(2,1)S(1)}, bf16[512]{0:T(512)(128)(2,1)S(1)}) all-reduce(bf16[512]{0:T(512)(128)(2,1)S(1)} %dynamic-update-slice.1, bf16[512]{0:T(512)(128)(2,1)S(1)} %dynamic-update-slice, ...), channel_id=1, replica_groups=mesh['expert'=4,'fsdp'=8] {'fsdp'}, use_global_device_ids=true, to_apply=%add.4 | all-reduce | flops 2048 | bytes 8192
  30.5 8.1 all-gather
  44.7 3.6 mul.290
  48.4 5.4 mul.291
  53.9 8.8 scatter_custom_fusion
  62.7 10.8 %all_gather.32 = bf16[512,512]{1,0:T(8,128)(2,1)} all-gather(bf16[64,512]{1,0:T(8,128)(2,1)S(1)} %convert_element_type.210), channel_id=1, replica_groups=mesh['expert'=4,'fsdp'=8] {'fsdp'}, dimensions={0}, use_global_device_ids=true | all-gather | bytes 589824 | tf_op jit(solution)/shard_map/all_gather | solution.py:47
  74.3 3.0 convolution_convert_fusion
  77.3 4.9 reshape.293
  82.2 4.7 fusion.72
  89.1 3.2 copy.155
  108.7 10.3 %gather_fusion.2 = bf16[3152,512]{1,0:T(8,128)(2,1)} fusion(bf16[1577,512]{1,0:T(8,128)(2,1)S(1)} %concatenate.7, s32[4096]{0:T(1024)S(1)} %get-tuple-element.65), kind=kCustom, calls=%fused_computation.2 | custom fusion | bytes 6467904 | tf_op jit(solution)/shard_map/gather | solution.py:131
  118.9 2.7 reshape.216
  121.7 5.0 copy.127
  126.7 5.0 all-to-all-start.2
  132.7 10.2 %gather_fusion = bf16[3152,512]{1,0:T(8,128)(2,1)} fusion(bf16[789,512]{1,0:T(8,128)(2,1)S(1)} %concatenate.6, s32[4096]{0:T(1024)S(1)} %get-tuple-element.66), kind=kCustom, calls=%fused_computation | custom fusion | bytes 6467904 | tf_op jit(solution)/shard_map/gather | solution.py:97
  145.5 5.0 copy.122
  150.5 54.2 %all-to-all-done.2 = bf16[4,2,394,512]{3,1,2,0:T(2,128)(2,1)} async-done(((bf16[4,2,394,512]{3,1,2,0:T(2,128)(2,1)}), bf16[4,2,394,512]{3,1,2,0:T(2,128)(2,1)}, u32[]{:S(2)}, u32[]{:S(2)}) %all-to-all-start.2) | async-done | bytes 3227680 | tf_op jit(solution)/shard_map/all_to_all | solution.py:132
  204.7 3.7 all-to-all-start
  210.6 37.3 %slice_reduce_fusion.1 = (bf16[4,394,512]{2,1,0:T(8,128)(2,1)}, bf16[4,394,512]{2,1,0:T(8,128)(2,1)}) fusion(bf16[1,2,4,394,512]{4,1,3,2,0:T(2,128)(2,1)} %bitcast.21), kind=kLoop, calls=%fused_computation.51 | loop fusion | bytes 6455296 | tf_op jit(solution)/shard_map/slice | solution.py:144
  248.0 3.0 squeeze.50
  251.0 3.0 squeeze.51
  254.0 26.5 %all-to-all-done = bf16[4,2,394,512]{3,1,2,0:T(2,128)(2,1)S(1)} async-done(((bf16[4,2,394,512]{3,1,2,0:T(2,128)(2,1)}), bf16[4,2,394,512]{3,1,2,0:T(2,128)(2,1)S(1)}, u32[]{:S(2)}, u32[]{:S(2)}) %all-to-all-start) | async-done | bytes 3227680 | tf_op jit(solution)/shard_map/all_to_all | solution.py:98
  280.6 36.0 %slice_reduce_fusion.3 = (bf16[4,394,512]{2,1,0:T(8,128)(2,1)}, bf16[4,394,512]{2,1,0:T(8,128)(2,1)}) fusion(bf16[1,2,4,394,512]{4,1,3,2,0:T(2,128)(2,1)S(1)} %bitcast.150), kind=kLoop, calls=%fused_computation.53 | loop fusion | bytes 6455296 | tf_op jit(solution)/shard_map/slice | solution.py:105
  320.2 32.9 %multiply_convert_fusion = (bf16[1576,2048]{1,0:T(8,128)(2,1)}, f32[1576,2048]{1,0:T(8,128)}, f32[1576,2048]{1,0:T(8,128)}) fusion(bf16[1576,512]{1,0:T(8,128)(2,1)} %squeeze.47, bf16[2,512,2048]{2,1,0:T(8,128)(2,1)} %all-gather.7.cloned.1.call-done), kind=kOutput, calls=%fused_computation.11 | convolution fusion | flops 3514908672 | bytes 35987456 | tf_op jit(solution)/shard_map/dot_general | solution.py:105
  353.2 15.5 %add_convert_fusion = bf16[1576,2048]{1,0:T(8,128)(2,1)} fusion(f32[1576,2048]{1,0:T(8,128)} %get-tuple-element.44, f32[1576,2048]{1,0:T(8,128)} %get-tuple-element.57, bf16[1576,512]{1,0:T(8,128)(2,1)S(1)} %copy-done.26, bf16[2,2048,512]{2,1,0:T(8,128)(2,1)} %all-gather.9.cloned.1.call-done), kind=kOutput, calls=%fused_computation.9 | convolution fusion | flops 3350298624 | bytes 35987456 | tf_op jit(solution)/shard_map/dot_general | solution.py:143
  368.6 6.4 fusion.16
  375.1 32.5 %multiply_convert_fusion.1 = (bf16[1576,2048]{1,0:T(8,128)(2,1)}, f32[1576,2048]{1,0:T(8,128)}, f32[1576,2048]{1,0:T(8,128)}) fusion(bf16[1576,512]{1,0:T(8,128)(2,1)S(1)} %squeeze.44, bf16[2,512,2048]{2,1,0:T(8,128)(2,1)S(1)} %copy-done.62), kind=kOutput, calls=%fused_computation.24 | convolution fusion | flops 3514908672 | bytes 35987456 | tf_op jit(solution)/shard_map/dot_general | solution.py:105
  407.6 15.6 %add_convert_fusion.1 = bf16[1576,2048]{1,0:T(8,128)(2,1)} fusion(f32[1576,2048]{1,0:T(8,128)} %get-tuple-element.42, f32[1576,2048]{1,0:T(8,128)} %get-tuple-element.60, bf16[1576,512]{1,0:T(8,128)(2,1)S(1)} %copy-done.24, bf16[2,2048,512]{2,1,0:T(8,128)(2,1)} %all-gather.9.cloned.1.call-done), kind=kOutput, calls=%fused_computation.10 | convolution fusion | flops 3350298624 | bytes 35987456 | tf_op jit(solution)/shard_map/dot_general | solution.py:143
  423.2 6.4 fusion.15
  429.9 11.9 %copy.128 = bf16[1,2,1576,512]{3,1,0,2:T(2,128)(2,1)} copy(bf16[1,2,1576,512]{3,2,1,0:T(8,128)(2,1)S(1)} %maximum_bitcast_fusion.1) | data formatting | bytes 6455296 | tf_op jit(solution)/shard_map/reshape | solution.py:157
  441.8 3.9 all-to-all-start.3
  445.7 7.1 fusion.14
  452.8 6.4 fusion.13
  459.5 11.9 %copy.123 = bf16[1,2,1576,512]{3,1,0,2:T(2,128)(2,1)} copy(bf16[1,2,1576,512]{3,2,1,0:T(8,128)(2,1)S(1)} %maximum_bitcast_fusion) | data formatting | bytes 6455296 | tf_op jit(solution)/shard_map/reshape | solution.py:114
  471.4 46.3 %all-to-all-done.3 = bf16[1,2,1576,512]{3,1,0,2:T(2,128)(2,1)S(1)} async-done(((bf16[1,2,1576,512]{3,1,0,2:T(2,128)(2,1)}), bf16[1,2,1576,512]{3,1,0,2:T(2,128)(2,1)S(1)}, u32[]{:S(2)}, u32[]{:S(2)}) %all-to-all-start.3) | async-done | bytes 3227680 | tf_op jit(solution)/shard_map/all_to_all | solution.py:158
  517.7 4.7 all-to-all-start.1
  527.4 2.6 reshape.218
  530.0 64.4 %all-to-all-done.1 = bf16[1,2,1576,512]{3,1,0,2:T(2,128)(2,1)} async-done(((bf16[1,2,1576,512]{3,1,0,2:T(2,128)(2,1)}), bf16[1,2,1576,512]{3,1,0,2:T(2,128)(2,1)}, u32[]{:S(2)}, u32[]{:S(2)}) %all-to-all-start.1) | async-done | bytes 3227680 | tf_op jit(solution)/shard_map/all_to_all | solution.py:115
  598.8 3.6 reshape.215
  602.3 6.0 gather_fusion.3
  608.3 8.4 gather_fusion.1
  616.8 3.6 reshape.221
  620.5 9.9 %multiply_reduce_fusion.2 = (f32[788,2]{1,0:T(8,128)}, f32[788,512]{1,0:T(8,128)}) fusion(f32[788,2,512]{2,1,0:T(2,128)S(1)} %reshape.221, f32[788,512]{1,0:T(8,128)} %convert_element_type.227, f32[788,2]{1,0:T(8,128)} %copy.118), kind=kLoop, calls=%fused_computation.56 | loop fusion | flops 2822616 | bytes 6467904 | tf_op jit(solution)/shard_map/reduce_sum | solution.py:124
  631.7 5.4 reshape.222
  637.1 5.8 reduce_sum.242
  654.8 4.2 fusion.35
  659.1 7.3 multiply_reduce_fusion
  666.7 6.4 multiply_convert_fusion.2
  675.8 4.5 copy.138
  680.3 6.8 convert_element_type.239
  687.2 5.2 convolution_convert_fusion.5
  692.4 8.9 fusion.18
  701.3 8.2 fusion.17
  710.6 4.7 pad_maximum_fusion
  715.6 7.4 fusion.20
  723.0 7.5 fusion.19
  733.6 4.3 fusion.68
  740.1 12.1 %all-reduce.11 = (bf16[512]{0:T(512)(128)(2,1)S(1)}, bf16[512]{0:T(512)(128)(2,1)S(1)}, bf16[512]{0:T(512)(128)(2,1)S(1)}, bf16[512]{0:T(512)(128)(2,1)S(1)}) all-reduce(bf16[512]{0:T(512)(128)(2,1)S(1)} %get-tuple-element.19, bf16[512]{0:T(512)(128)(2,1)S(1)} %get-tuple-element.22, ...), channel_id=2, replica_groups=mesh['expert'=4,'fsdp'=8] {'fsdp'}, use_global_device_ids=true, to_apply=%region_24.25.clone | all-reduce | flops 2048 | bytes 8192
  752.5 3.2 add_add_fusion.2
  755.7 21.6 %reduce-scatter.16.cloned.1.call-done = bf16[64,8]{1,0:T(8,128)(2,1)} async-done(((bf16[512,8]{1,0:T(8,128)(2,1)}), bf16[64,8]{1,0:T(8,128)(2,1)}) %reduce-scatter.16.cloned.1.call-update) | async-done | bytes 1040
  778.1 11.7 %all-reduce.13 = (bf16[64]{0:T(256)(128)(2,1)S(1)}, bf16[64]{0:T(256)(128)(2,1)S(1)}, bf16[64]{0:T(256)(128)(2,1)S(1)}, bf16[64]{0:T(256)(128)(2,1)S(1)}, bf16[64,8]{0,1:T(8,128)(2,1)S(1)}) all-reduce(bf16[64]{0:T(256)(128)(2,1)S(1)} %dynamic-slice.5, ...), channel_id=1, replica_groups=mesh['expert'=4,'fsdp'=8] {'expert'}, use_global_device_ids=true, to_apply=%region_25.26 | all-reduce | flops 768 | bytes 3072 | tf_op jit(solution)/shard_map/psum | solution.py:247
  792.5 39.4 %reduce-scatter.12.cloned.1.call-done = bf16[2,64,2048]{2,1,0:T(8,128)(2,1)} async-done(((bf16[2,512,2048]{2,1,0:T(8,128)(2,1)}), bf16[2,64,2048]{2,1,0:T(8,128)(2,1)}) %reduce-scatter.12.cloned.1.call-update) | async-done | bytes 524304 | tf_op jit(solution)/shard_map/reduce_scatter | solution.py:168
  834.0 52.4 %reduce-scatter.14.cloned.1.call-done = bf16[2,256,512]{2,1,0:T(8,128)(2,1)} async-done(((bf16[2,2048,512]{2,1,0:T(8,128)(2,1)}), bf16[2,256,512]{2,1,0:T(8,128)(2,1)}) %reduce-scatter.14.cloned.1.call-update) | async-done | bytes 524304 | tf_op jit(solution)/shard_map/reduce_scatter | solution.py:171
  888.5 35.9 %all-reduce.17.cloned.1.call-done = (bf16[64,1536]{1,0:T(8,128)(2,1)}, bf16[64,512]{1,0:T(8,128)(2,1)}) async-done(((bf16[64,1536]{1,0:T(8,128)(2,1)}, bf16[64,512]{1,0:T(8,128)(2,1)}), (bf16[64,1536]{1,0:T(8,128)(2,1)}, bf16[64,512]{1,0:T(8,128)(2,1)})) %all-reduce.17.cloned.1.call-update) | async-done | bytes 262160 | tf_op jit(solution)/shard_map/psum | solution.py:249
  (265 shorter events, 85.2 us)
Async XLA Ops:
  7.2 67.1 %all-gather.5.cloned.1.call-start = ((), (), s32[]{:S(2)}) async-start(), calls=%async_computation.9 | async-start | bytes 1769472 | tf_op jit(solution)/shard_map/all_gather | solution.py:46
  30.4 43.9 %copy-start.60 = (f32[512]{0:T(512)}, f32[512]{0:T(512)S(1)}, u32[]{:S(2)}) copy-start(f32[512]{0:T(512)S(1)} %convert_element_type.203) | copy-start | bytes 6148
  30.4 43.9 %copy-start.58 = (f32[512]{0:T(512)}, f32[512]{0:T(512)S(1)}, u32[]{:S(2)}) copy-start(f32[512]{0:T(512)S(1)} %convert_element_type.201) | copy-start | bytes 6148
  30.4 72.3 %copy-start.54 = (f32[512]{0:T(512)}, f32[512]{0:T(512)S(1)}, u32[]{:S(2)}) copy-start(f32[512]{0:T(512)S(1)} %convert_element_type.212) | copy-start | bytes 6148
  38.6 65.2 %copy-start.40 = (bf16[512,8]{0,1:T(8,128)(2,1)}, bf16[512,8]{0,1:T(8,128)(2,1)S(1)}, u32[]{:S(2)}) copy-start(bf16[512,8]{0,1:T(8,128)(2,1)S(1)} %reshape.278) | copy-start | bytes 24580
  48.4 25.2 %copy-start.3 = (bf16[788,512]{1,0:T(8,128)(2,1)S(1)}, bf16[788,512]{1,0:T(8,128)(2,1)}, u32[]{:S(2)}) copy-start(bf16[788,512]{1,0:T(8,128)(2,1)} %param.12) | copy-start | bytes 2420740
  53.8 8.9 copy-start.56
  73.8 3.5 copy-start.46
  74.2 3.1 copy-start.48
  74.2 3.1 copy-start.52
  89.1 6.4 copy-start.11
  95.5 3.4 copy-start
  99.0 2.6 copy-start.22
  101.6 4.1 copy-start.34
  102.3 5.6 copy-start.8
  102.3 3.4 copy-start.36
  102.7 2.4 copy-start.50
  103.5 4.8 copy-start.42
  105.7 3.0 copy-start.44
  126.7 5.0 copy-start.29
  126.7 5.9 copy-start.6
  126.7 78.1 %all-to-all-start.2 = ((bf16[4,2,394,512]{3,1,2,0:T(2,128)(2,1)}), bf16[4,2,394,512]{3,1,2,0:T(2,128)(2,1)}, u32[]{:S(2)}, u32[]{:S(2)}) async-start(bf16[4,2,394,512]{3,1,2,0:T(2,128)(2,1)} %copy.127), calls=%async_computation.2 | async-start | bytes 6455296 | tf_op jit(solution)/shard_map/all_to_all | solution.py:132
  131.6 188.6 %all-gather.7.cloned.1.call-start = ((), (), s32[]{:S(2)}) async-start(), calls=%async_computation.10 | async-start | bytes 4718592 | tf_op jit(solution)/shard_map/all_gather | solution.py:53
  204.7 75.8 %all-to-all-start = ((bf16[4,2,394,512]{3,1,2,0:T(2,128)(2,1)}), bf16[4,2,394,512]{3,1,2,0:T(2,128)(2,1)S(1)}, u32[]{:S(2)}, u32[]{:S(2)}) async-start(bf16[4,2,394,512]{3,1,2,0:T(2,128)(2,1)} %copy.122), calls=%async_computation | async-start | bytes 6455296 | tf_op jit(solution)/shard_map/all_to_all | solution.py:98
  208.5 144.7 %all-gather.9.cloned.1.call-start = ((), (), s32[]{:S(2)}) async-start(), calls=%async_computation.11 | async-start | bytes 4718592 | tf_op jit(solution)/shard_map/all_gather | solution.py:54
  318.5 56.5 %copy-start.27 = (bf16[1576,512]{1,0:T(8,128)(2,1)}, bf16[1576,512]{1,0:T(8,128)(2,1)S(1)}, u32[]{:S(2)}) copy-start(bf16[1576,512]{1,0:T(8,128)(2,1)S(1)} %squeeze.44) | copy-start | bytes 4841476
  320.2 32.9 %copy-start.26 = (bf16[1576,512]{1,0:T(8,128)(2,1)S(1)}, bf16[1576,512]{1,0:T(8,128)(2,1)}, u32[]{:S(2)}) copy-start(bf16[1576,512]{1,0:T(8,128)(2,1)} %squeeze.51) | copy-start | bytes 4841476
  353.1 15.5 %copy-start.62 = (bf16[2,512,2048]{2,1,0:T(8,128)(2,1)S(1)}, bf16[2,512,2048]{2,1,0:T(8,128)(2,1)}, u32[]{:S(2)}) copy-start(bf16[2,512,2048]{2,1,0:T(8,128)(2,1)} %all-gather.7.cloned.1.call-done) | copy-start | bytes 12582916
  375.1 32.5 %copy-start.24 = (bf16[1576,512]{1,0:T(8,128)(2,1)S(1)}, bf16[1576,512]{1,0:T(8,128)(2,1)}, u32[]{:S(2)}) copy-start(bf16[1576,512]{1,0:T(8,128)(2,1)} %squeeze.50) | copy-start | bytes 4841476
  441.8 75.9 %all-to-all-start.3 = ((bf16[1,2,1576,512]{3,1,0,2:T(2,128)(2,1)}), bf16[1,2,1576,512]{3,1,0,2:T(2,128)(2,1)S(1)}, u32[]{:S(2)}, u32[]{:S(2)}) async-start(bf16[1,2,1576,512]{3,1,0,2:T(2,128)(2,1)} %copy.128), calls=%async_computation.3 | async-start | bytes 6455296 | tf_op jit(solution)/shard_map/all_to_all | solution.py:158
  445.7 7.2 copy-start.63
  471.4 53.5 %copy-start.57 = (s32[1576]{0:T(1024)S(1)}, s32[1576]{0:T(1024)}, u32[]{:S(2)}) copy-start(s32[1576]{0:T(1024)} %copy-done.56) | copy-start | bytes 18916
  517.7 76.7 %all-to-all-start.1 = ((bf16[1,2,1576,512]{3,1,0,2:T(2,128)(2,1)}), bf16[1,2,1576,512]{3,1,0,2:T(2,128)(2,1)}, u32[]{:S(2)}, u32[]{:S(2)}) async-start(bf16[1,2,1576,512]{3,1,0,2:T(2,128)(2,1)} %copy.123), calls=%async_computation.1 | async-start | bytes 6455296 | tf_op jit(solution)/shard_map/all_to_all | solution.py:115
  522.3 230.2 %reduce-scatter.10.cloned.1.call-start = ((), (), s32[]{:S(2)}) async-start(), calls=%async_computation.13 | async-start | bytes 589824 | tf_op jit(solution)/shard_map/reduce_scatter | solution.py:233
  620.4 11.1 %copy-start.35 = (s32[788,2]{0,1:T(2,128)S(1)}, s32[788,2]{0,1:T(2,128)}, u32[]{:S(2)}) copy-start(s32[788,2]{0,1:T(2,128)} %param.13) | copy-start | bytes 18916
  620.4 11.1 %copy-start.33 = (f32[788,8]{0,1:T(8,128)S(1)}, f32[788,8]{0,1:T(8,128)}, u32[]{:S(2)}) copy-start(f32[788,8]{0,1:T(8,128)} %copy-done.32) | copy-start | bytes 75652
  620.4 11.1 %copy-start.39 = (f32[788]{0:T(1024)S(1)}, f32[788]{0:T(1024)}, u32[]{:S(2)}) copy-start(f32[788]{0:T(1024)} %copy-done.38) | copy-start | bytes 9460
  620.5 11.1 %copy-start.45 = (f32[788]{0:T(1024)S(1)}, f32[788]{0:T(1024)}, u32[]{:S(2)}) copy-start(f32[788]{0:T(1024)} %copy-done.44) | copy-start | bytes 9460
  631.6 11.2 %copy-start.2 = (f32[788,512]{1,0:T(8,128)S(1)}, f32[788,512]{1,0:T(8,128)}, u32[]{:S(2)}) copy-start(f32[788,512]{1,0:T(8,128)} %copy-done.1) | copy-start | bytes 4841476
  631.7 11.2 %copy-start.37 = (f32[788]{0:T(1024)S(1)}, f32[788]{0:T(1024)}, u32[]{:S(2)}) copy-start(f32[788]{0:T(1024)} %copy-done.36) | copy-start | bytes 9460
  631.7 11.2 %copy-start.41 = (bf16[512,8]{0,1:T(8,128)(2,1)S(1)}, bf16[512,8]{0,1:T(8,128)(2,1)}, u32[]{:S(2)}) copy-start(bf16[512,8]{0,1:T(8,128)(2,1)} %copy-done.40) | copy-start | bytes 24580
  631.7 11.2 %copy-start.43 = (f32[788]{0:T(1024)S(1)}, f32[788]{0:T(1024)}, u32[]{:S(2)}) copy-start(f32[788]{0:T(1024)} %copy-done.42) | copy-start | bytes 9460
  631.7 11.2 %copy-start.55 = (f32[512]{0:T(512)S(1)}, f32[512]{0:T(512)}, u32[]{:S(2)}) copy-start(f32[512]{0:T(512)} %copy-done.54) | copy-start | bytes 6148
  637.1 6.8 copy-start.51
  643.9 3.2 copy-start.15
  643.9 3.2 copy-start.21
  644.4 4.3 copy-start.23
  648.7 6.1 copy-start.31
  654.8 4.3 copy-start.14
  666.5 86.0 %reduce-scatter.8.cloned.1.call-start = ((), (), s32[]{:S(2)}) async-start(), calls=%async_computation.12 | async-start | bytes 1769472 | tf_op jit(solution)/shard_map/reduce_scatter | solution.py:230
  666.7 6.4 copy-start.12
  680.3 6.8 copy-start.4
  680.3 6.8 copy-start.47
  680.3 6.8 copy-start.53
  680.3 6.8 copy-start.59
  680.3 6.8 copy-start.61
  692.4 85.0 %reduce-scatter.16.cloned.1.call-start = ((), (), s32[]{:S(2)}) async-start(), calls=%async_computation.16 | async-start | bytes 147456
  692.4 8.9 copy-start.28
  701.3 8.2 copy-start.7
  710.5 121.3 %reduce-scatter.12.cloned.1.call-start = ((), (), s32[]{:S(2)}) async-start(), calls=%async_computation.14 | async-start | bytes 4718592 | tf_op jit(solution)/shard_map/reduce_scatter | solution.py:168
  715.3 171.0 %reduce-scatter.14.cloned.1.call-start = ((), (), s32[]{:S(2)}) async-start(), calls=%async_computation.15 | async-start | bytes 4718592 | tf_op jit(solution)/shard_map/reduce_scatter | solution.py:171
  715.6 7.4 copy-start.25
  732.9 191.5 %all-reduce.17.cloned.1.call-start = ((), (), s32[]{:S(2)}) async-start(), calls=%async_computation.17 | async-start | bytes 524288 | tf_op jit(solution)/shard_map/psum | solution.py:249
  733.6 4.3 copy-start.49
  (13 other events, 15.9 us)
Sparse Core Ops, SparseCore 0:
  10.4 28.3 all-gather.4
  134.9 37.0 all-gather.6
  211.2 37.0 all-gather.8
  666.6 32.2 reduce-scatter.9
  702.0 38.3 reduce-scatter.7
  743.8 33.5 reduce-scatter.15
  780.7 51.1 reduce-scatter.11
  835.2 51.0 reduce-scatter.13
  888.7 35.6 all-reduce.16
where the time goes:
time: 945 us; the launch traced here: 935 us
  waiting for transfers between devices  341 us (36%)
  local copies, waits for them, and re-layouts  248 us (26%)
  matrix products  189 us (20%)
  other arithmetic  64 us (7%)
  blocking collectives  57.9 us (6%)
  starting transfers between devices  18 us (2%)
  between operations  16.7 us (2%)
    dot_general x2, matrix products, local(): jnp.dot(arrived[member], up_full[member], preferred_element_type=jnp.floa...  65.4 us
    all_to_all x1, waiting for transfers between devices, local(): lax.all_to_all(expert_out, 'expert', split_axis=2, concat_axis=0, tiled=T...  64.4 us
    all_to_all x1, waiting for transfers between devices, local(): lax.all_to_all(outgoing_grad, 'expert', split_axis=0, concat_axis=2, tile...  54.2 us
    reduce_scatter x1, waiting for transfers between devices, local(): lax.psum_scatter(down_total.astype(jnp.bfloat16), 'fsdp', scatter_dimensi...  52.4 us
    all_to_all x1, waiting for transfers between devices, local(): lax.all_to_all(row_grad, 'expert', split_axis=2, concat_axis=0, tiled=True)  46.3 us
    reduce_scatter x1, waiting for transfers between devices, local(): lax.psum_scatter(up_total.astype(jnp.bfloat16), 'fsdp', scatter_dimension...  39.4 us
    slice x1, local copies, waits for them, and re-layouts, local(): arrived_grad[member]  37.3 us
    slice x1, local copies, waits for them, and re-layouts, local(): arrived[member]  36 us
  transfers between devices with their start and end apart: 13, of which 8 were waited for; matrix products, arithmetic and copies ran while one was open for 30% of the time, Pallas kernels for 0%

commit v1 on v0

--- a/solution.py
+++ b/solution.py
@@ -112,7 +112,18 @@
             )
         )
     expert_out = jnp.stack(result_list, 0).reshape(1, per_owner, spread_rows, width)
-    returned = lax.all_to_all(expert_out, "expert", split_axis=2, concat_axis=0, tiled=True)
+    ways, here = (lax.axis_size("expert"), lax.axis_index("expert"))
+    width_2 = expert_out.shape[2] // ways
+    dims = list(expert_out.shape)
+    dims[2] = width_2
+    height = dims[0]
+    dims[0] = height * ways
+    returned = jnp.zeros(dims, expert_out.dtype)
+    for mask in range(ways):
+        part = lax.dynamic_slice_in_dim(expert_out, (here ^ mask) * width_2, width_2, axis=2)
+        if mask:
+            part = lax.ppermute(part, "expert", [(d, d ^ mask) for d in range(ways)])
+        returned = lax.dynamic_update_slice_in_dim(returned, part, (here ^ mask) * height, axis=0)
     pair_out = (
         returned.reshape(experts * capacity, width)[slots]
         .reshape(local_rows, TOP, width)

time: 945 us -> 908 us (0.961)
  waiting for transfers between devices: 341 us -> 301 us
  blocking collectives: 57.9 us -> 69.4 us
    ppermute x0 -> x3, waiting for transfers between devices: none -> 95 us  [local(): part = lax.ppermute(part, 'expert', [(d, d ^ mask) for d in range(ways)])]
    all_to_all x1 -> x0, waiting for transfers between devices: 64.4 us -> none  [local(): lax.all_to_all(expert_out, 'expert', split_axis=2, concat_axis=0, tiled=T...]
    all_to_all x1, waiting for transfers between devices: 46.3 us -> 0.01 us  [local(): lax.all_to_all(row_grad, 'expert', split_axis=2, concat_axis=0, tiled=True)]
    unnamed x10, waiting for transfers between devices: 21.8 us -> 0.17 us
    reshape x1 -> x0, local copies, waits for them, and re-layouts: 11.9 us -> none  [local(): jnp.stack(result_list, 0).reshape(1, per_owner, spread_rows, width)]
    psum x1, blocking collectives: 11.7 us -> 22.9 us  [local(): lax.psum(shares[0].astype(jnp.bfloat16), 'expert').astype(jnp.float32)]
    unnamed x149 -> x179, local copies, waits for them, and re-layouts: 19.6 us -> 21.5 us
  transfers between devices with their start and end apart: 13 -> 15, of which waited for: 8 -> 7; matrix products, arithmetic and copies ran while one was open for 30% -> 38% of each run, Pallas kernels for 0% -> 0%
where the time goes in v1:
time: 908 us; the launch traced here: 897 us
  waiting for transfers between devices  301 us (33%)
  local copies, waits for them, and re-layouts  242 us (27%)
  matrix products  188 us (21%)
  blocking collectives  69.4 us (8%)
  other arithmetic  61.6 us (7%)
  starting transfers between devices  18.5 us (2%)
  between operations  16.8 us (2%)
    ppermute x3, waiting for transfers between devices, local(): part = lax.ppermute(part, 'expert', [(d, d ^ mask) for d in range(ways)])  95 us
    dot_general x2, matrix products, local(): jnp.dot(arrived[member], up_full[member], preferred_element_type=jnp.floa...  65.4 us
    all_to_all x1, waiting for transfers between devices, local(): lax.all_to_all(outgoing_grad, 'expert', split_axis=0, concat_axis=2, tile...  54.2 us
    reduce_scatter x1, waiting for transfers between devices, local(): lax.psum_scatter(down_total.astype(jnp.bfloat16), 'fsdp', scatter_dimensi...  52.4 us
    slice x1, local copies, waits for them, and re-layouts, local(): arrived_grad[member]  37.4 us
    reduce_scatter x1, waiting for transfers between devices, local(): lax.psum_scatter(up_total.astype(jnp.bfloat16), 'fsdp', scatter_dimension...  36.9 us
    psum x1, waiting for transfers between devices, local(): lax.psum(shares[2].astype(jnp.bfloat16), 'expert').astype(jnp.float32)  35.9 us
    slice x1, local copies, waits for them, and re-layouts, local(): arrived[member]  35.9 us
  transfers between devices with their start and end apart: 15, of which 7 were waited for; matrix products, arithmetic and copies ran while one was open for 38% of the time, Pallas kernels for 0%

profile of v1, /device:TPU:0, one launch (start us, length us, event | category | flops | bytes accessed | tf_op | source)
XLA Modules:
  0.0 897.4 jit_solution(3017280288860091068)
XLA Ops:
  15.2 15.3 %all-reduce.12 = (bf16[512]{0:T(512)(128)(2,1)S(1)}, bf16[512]{0:T(512)(128)(2,1)S(1)}, bf16[512]{0:T(512)(128)(2,1)S(1)}, bf16[512]{0:T(512)(128)(2,1)S(1)}) all-reduce(bf16[512]{0:T(512)(128)(2,1)S(1)} %dynamic-update-slice.1, bf16[512]{0:T(512)(128)(2,1)S(1)} %dynamic-update-slice, ...), channel_id=1, replica_groups=mesh['expert'=4,'fsdp'=8] {'fsdp'}, use_global_device_ids=true, to_apply=%add.4 | all-reduce | flops 2048 | bytes 8192
  30.5 8.1 all-gather
  44.8 2.5 mul.306
  47.3 5.4 mul.307
  52.8 8.8 scatter_custom_fusion
  61.7 10.8 %all_gather.32 = bf16[512,512]{1,0:T(8,128)(2,1)} all-gather(bf16[64,512]{1,0:T(8,128)(2,1)S(1)} %convert_element_type.210), channel_id=1, replica_groups=mesh['expert'=4,'fsdp'=8] {'fsdp'}, dimensions={0}, use_global_device_ids=true | all-gather | bytes 589824 | tf_op jit(solution)/shard_map/all_gather | solution.py:47
  73.3 3.0 convolution_convert_fusion
  76.3 4.9 reshape.293
  81.2 4.7 fusion.81
  88.1 3.2 copy.188
  108.3 10.3 %gather_fusion.2 = bf16[3152,512]{1,0:T(8,128)(2,1)} fusion(bf16[1577,512]{1,0:T(8,128)(2,1)S(1)} %concatenate.7, s32[4096]{0:T(1024)S(1)} %get-tuple-element.68), kind=kCustom, calls=%fused_computation.2 | custom fusion | bytes 6467904 | tf_op jit(solution)/shard_map/gather | solution.py:142
  118.6 2.6 reshape.216
  121.2 5.0 copy.161
  126.2 5.0 all-to-all-start.1
  132.2 10.2 %gather_fusion = bf16[3152,512]{1,0:T(8,128)(2,1)} fusion(bf16[789,512]{1,0:T(8,128)(2,1)S(1)} %concatenate.6, s32[4096]{0:T(1024)S(1)} %get-tuple-element.69), kind=kCustom, calls=%fused_computation | custom fusion | bytes 6467904 | tf_op jit(solution)/shard_map/gather | solution.py:97
  142.5 2.5 reshape.214
  145.0 5.0 copy.153
  150.0 54.2 %all-to-all-done.1 = bf16[4,2,394,512]{3,1,2,0:T(2,128)(2,1)} async-done(((bf16[4,2,394,512]{3,1,2,0:T(2,128)(2,1)}), bf16[4,2,394,512]{3,1,2,0:T(2,128)(2,1)}, u32[]{:S(2)}, u32[]{:S(2)}) %all-to-all-start.1) | async-done | bytes 3227680 | tf_op jit(solution)/shard_map/all_to_all | solution.py:143
  204.2 3.7 all-to-all-start
  210.1 37.4 %slice_reduce_fusion.1 = (bf16[4,394,512]{2,1,0:T(8,128)(2,1)}, bf16[4,394,512]{2,1,0:T(8,128)(2,1)}) fusion(bf16[1,2,4,394,512]{4,1,3,2,0:T(2,128)(2,1)} %bitcast.22), kind=kLoop, calls=%fused_computation.58 | loop fusion | bytes 6455296 | tf_op jit(solution)/shard_map/slice | solution.py:155
  247.6 3.0 squeeze.50
  250.6 3.1 squeeze.51
  253.7 26.4 %all-to-all-done = bf16[4,2,394,512]{3,1,2,0:T(2,128)(2,1)S(1)} async-done(((bf16[4,2,394,512]{3,1,2,0:T(2,128)(2,1)}), bf16[4,2,394,512]{3,1,2,0:T(2,128)(2,1)S(1)}, u32[]{:S(2)}, u32[]{:S(2)}) %all-to-all-start) | async-done | bytes 3227680 | tf_op jit(solution)/shard_map/all_to_all | solution.py:98
  280.0 35.9 %slice_reduce_fusion.2 = (bf16[4,394,512]{2,1,0:T(8,128)(2,1)}, bf16[4,394,512]{2,1,0:T(8,128)(2,1)}) fusion(bf16[1,2,4,394,512]{4,1,3,2,0:T(2,128)(2,1)S(1)} %bitcast.154), kind=kLoop, calls=%fused_computation.59 | loop fusion | bytes 6455296 | tf_op jit(solution)/shard_map/slice | solution.py:105
  319.7 32.9 %multiply_convert_fusion.1 = (bf16[1576,2048]{1,0:T(8,128)(2,1)}, f32[1576,2048]{1,0:T(8,128)}, f32[1576,2048]{1,0:T(8,128)}) fusion(bf16[1576,512]{1,0:T(8,128)(2,1)} %squeeze.44, bf16[2,512,2048]{2,1,0:T(8,128)(2,1)} %all-gather.7.cloned.1.call-done), kind=kOutput, calls=%fused_computation.24 | convolution fusion | flops 3514908672 | bytes 35987456 | tf_op jit(solution)/shard_map/dot_general | solution.py:105
  352.6 15.5 %add_convert_fusion.1 = bf16[1576,2048]{1,0:T(8,128)(2,1)} fusion(f32[1576,2048]{1,0:T(8,128)} %get-tuple-element.44, f32[1576,2048]{1,0:T(8,128)} %get-tuple-element.63, bf16[1576,512]{1,0:T(8,128)(2,1)S(1)} %copy-done.35, bf16[2,2048,512]{2,1,0:T(8,128)(2,1)} %all-gather.9.cloned.1.call-done), kind=kOutput, calls=%fused_computation.10 | convolution fusion | flops 3350298624 | bytes 35987456 | tf_op jit(solution)/shard_map/dot_general | solution.py:154
  368.0 6.4 fusion.15
  374.5 32.5 %multiply_convert_fusion = (bf16[1576,2048]{1,0:T(8,128)(2,1)}, f32[1576,2048]{1,0:T(8,128)}, f32[1576,2048]{1,0:T(8,128)}) fusion(bf16[1576,512]{1,0:T(8,128)(2,1)S(1)} %squeeze.47, bf16[2,512,2048]{2,1,0:T(8,128)(2,1)S(1)} %copy-done.74), kind=kOutput, calls=%fused_computation.11 | convolution fusion | flops 3514908672 | bytes 35987456 | tf_op jit(solution)/shard_map/dot_general | solution.py:105
  407.0 15.1 %add_convert_fusion = bf16[1576,2048]{1,0:T(8,128)(2,1)} fusion(f32[1576,2048]{1,0:T(8,128)} %get-tuple-element.42, f32[1576,2048]{1,0:T(8,128)} %get-tuple-element.60, bf16[1576,512]{1,0:T(8,128)(2,1)S(1)} %copy-done.37, bf16[2,2048,512]{2,1,0:T(8,128)(2,1)} %all-gather.9.cloned.1.call-done), kind=kOutput, calls=%fused_computation.9 | convolution fusion | flops 3350298624 | bytes 35987456 | tf_op jit(solution)/shard_map/dot_general | solution.py:154
  422.1 6.4 fusion.16
  428.9 11.9 %copy.162 = bf16[1,2,1576,512]{3,1,0,2:T(2,128)(2,1)} copy(bf16[1,2,1576,512]{3,2,1,0:T(8,128)(2,1)S(1)} %maximum_bitcast_fusion) | data formatting | bytes 6455296 | tf_op jit(solution)/shard_map/reshape | solution.py:168
  440.7 4.7 all-to-all-start.2
  445.9 7.1 fusion.13
  453.0 6.4 fusion.14
  465.3 2.4 collective-permute-start.1
  473.2 42.8 %collective-permute-done = bf16[1,2,394,512]{3,1,2,0:T(2,128)(2,1)} collective-permute-done((bf16[1,2,394,512]{3,1,2,0:T(2,128)(2,1)}, bf16[1,2,394,512]{3,1,2,0:T(2,128)(2,1)}, u32[]{:S(2)}, u32[]{:S(2)}) %collective-permute-start) | collective-permute-done | bytes 806944 | tf_op jit(solution)/shard_map/ppermute | solution.py:125
  518.1 52.2 %collective-permute-done.1 = bf16[1,2,394,512]{3,1,2,0:T(2,128)(2,1)} collective-permute-done((bf16[1,2,394,512]{3,1,2,0:T(2,128)(2,1)}, bf16[1,2,394,512]{3,1,2,0:T(2,128)(2,1)}, u32[]{:S(2)}, u32[]{:S(2)}) %collective-permute-start.1) | collective-permute-done | bytes 806944 | tf_op jit(solution)/shard_map/ppermute | solution.py:125
  574.6 2.5 reshape.215
  577.1 6.0 gather_fusion.1
  583.1 5.1 reshape.221
  588.2 11.3 %multiply_reduce_fusion.2 = (f32[788,2]{1,0:T(8,128)S(1)}, f32[788,512]{1,0:T(8,128)}) fusion(f32[788,2,512]{2,1,0:T(2,128)} %reshape.221, f32[788,512]{1,0:T(8,128)S(1)} %copy-done.24, f32[788,2]{1,0:T(8,128)S(1)} %copy-done.32), kind=kLoop, calls=%fused_computation.62 | loop fusion | flops 2822616 | bytes 6467904 | tf_op jit(solution)/shard_map/reduce_sum | solution.py:135
  601.0 2.5 copy.197
  605.4 2.6 reshape.218
  607.9 6.0 gather_fusion.3
  614.0 4.9 reshape.222
  618.9 5.9 reduce_sum.242
  631.9 5.3 fusion.35
  637.2 7.5 multiply_reduce_fusion
  644.6 4.6 multiply_convert_fusion.2
  656.1 4.5 copy.172
  660.6 7.2 convert_element_type.239
  667.8 5.2 convolution_convert_fusion.5
  673.1 7.6 fusion.17
  680.7 7.2 fusion.18
  691.6 7.8 fusion.19
  699.4 7.5 fusion.20
  706.9 2.3 pad_maximum_fusion.1
  710.9 3.9 fusion.77
  716.8 12.3 %all-reduce.11 = (bf16[512]{0:T(512)(128)(2,1)S(1)}, bf16[512]{0:T(512)(128)(2,1)S(1)}, bf16[512]{0:T(512)(128)(2,1)S(1)}, bf16[512]{0:T(512)(128)(2,1)S(1)}) all-reduce(bf16[512]{0:T(512)(128)(2,1)S(1)} %get-tuple-element.19, bf16[512]{0:T(512)(128)(2,1)S(1)} %get-tuple-element.22, ...), channel_id=2, replica_groups=mesh['expert'=4,'fsdp'=8] {'fsdp'}, use_global_device_ids=true, to_apply=%region_24.25.clone | all-reduce | flops 2048 | bytes 8192
  729.4 22.9 %all-reduce.13 = (bf16[64]{0:T(256)(128)(2,1)S(1)}, bf16[64]{0:T(256)(128)(2,1)S(1)}, bf16[64]{0:T(256)(128)(2,1)S(1)}, bf16[64]{0:T(256)(128)(2,1)S(1)}, bf16[64,8]{0,1:T(8,128)(2,1)S(1)}) all-reduce(bf16[64]{0:T(256)(128)(2,1)S(1)} %dynamic-slice.21, ...), channel_id=1, replica_groups=mesh['expert'=4,'fsdp'=8] {'expert'}, use_global_device_ids=true, to_apply=%region_25.26 | all-reduce | flops 768 | bytes 3072 | tf_op jit(solution)/shard_map/psum | solution.py:258
  755.0 3.0 add_add_fusion.2
  758.1 36.9 %reduce-scatter.12.cloned.1.call-done = bf16[2,64,2048]{2,1,0:T(8,128)(2,1)} async-done(((bf16[2,512,2048]{2,1,0:T(8,128)(2,1)}), bf16[2,64,2048]{2,1,0:T(8,128)(2,1)}) %reduce-scatter.12.cloned.1.call-update) | async-done | bytes 524304 | tf_op jit(solution)/shard_map/reduce_scatter | solution.py:179
  797.1 52.4 %reduce-scatter.14.cloned.1.call-done = bf16[2,256,512]{2,1,0:T(8,128)(2,1)} async-done(((bf16[2,2048,512]{2,1,0:T(8,128)(2,1)}), bf16[2,256,512]{2,1,0:T(8,128)(2,1)}) %reduce-scatter.14.cloned.1.call-update) | async-done | bytes 524304 | tf_op jit(solution)/shard_map/reduce_scatter | solution.py:182
  851.6 35.9 %all-reduce.17.cloned.1.call-done = (bf16[64,1536]{1,0:T(8,128)(2,1)}, bf16[64,512]{1,0:T(8,128)(2,1)}) async-done(((bf16[64,1536]{1,0:T(8,128)(2,1)}, bf16[64,512]{1,0:T(8,128)(2,1)}), (bf16[64,1536]{1,0:T(8,128)(2,1)}, bf16[64,512]{1,0:T(8,128)(2,1)})) %all-reduce.17.cloned.1.call-update) | async-done | bytes 262160 | tf_op jit(solution)/shard_map/psum | solution.py:260
  (305 shorter events, 92.9 us)
Async XLA Ops:
  7.2 37.6 %copy-start.14 = (bf16[788,512]{1,0:T(8,128)(2,1)S(1)}, bf16[788,512]{1,0:T(8,128)(2,1)}, u32[]{:S(2)}) copy-start(bf16[788,512]{1,0:T(8,128)(2,1)} %param.14) | copy-start | bytes 2420740
  7.2 66.1 %all-gather.5.cloned.1.call-start = ((), (), s32[]{:S(2)}) async-start(), calls=%async_computation.8 | async-start | bytes 1769472 | tf_op jit(solution)/shard_map/all_gather | solution.py:46
  30.5 42.8 %copy-start.72 = (f32[512]{0:T(512)}, f32[512]{0:T(512)S(1)}, u32[]{:S(2)}) copy-start(f32[512]{0:T(512)S(1)} %convert_element_type.203) | copy-start | bytes 6148
  30.5 42.8 %copy-start.70 = (f32[512]{0:T(512)}, f32[512]{0:T(512)S(1)}, u32[]{:S(2)}) copy-start(f32[512]{0:T(512)S(1)} %convert_element_type.201) | copy-start | bytes 6148
  30.5 71.9 %copy-start.66 = (f32[512]{0:T(512)}, f32[512]{0:T(512)S(1)}, u32[]{:S(2)}) copy-start(f32[512]{0:T(512)S(1)} %convert_element_type.212) | copy-start | bytes 6148
  38.7 64.8 %copy-start.52 = (bf16[512,8]{0,1:T(8,128)(2,1)}, bf16[512,8]{0,1:T(8,128)(2,1)S(1)}, u32[]{:S(2)}) copy-start(bf16[512,8]{0,1:T(8,128)(2,1)S(1)} %reshape.278) | copy-start | bytes 24580
  47.3 25.2 %copy-start.3 = (bf16[788,512]{1,0:T(8,128)(2,1)S(1)}, bf16[788,512]{1,0:T(8,128)(2,1)}, u32[]{:S(2)}) copy-start(bf16[788,512]{1,0:T(8,128)(2,1)} %param.12) | copy-start | bytes 2420740
  52.8 8.9 copy-start.68
  72.7 3.5 copy-start.58
  73.2 3.1 copy-start.60
  88.1 6.4 copy-start.10
  102.0 3.4 copy-start.46
  102.0 5.6 copy-start.8
  102.0 3.3 copy-start.48
  103.2 4.7 copy-start.54
  126.2 5.0 copy-start.41
  126.2 5.9 copy-start.6
  126.2 78.1 %all-to-all-start.1 = ((bf16[4,2,394,512]{3,1,2,0:T(2,128)(2,1)}), bf16[4,2,394,512]{3,1,2,0:T(2,128)(2,1)}, u32[]{:S(2)}, u32[]{:S(2)}) async-start(bf16[4,2,394,512]{3,1,2,0:T(2,128)(2,1)} %copy.161), calls=%async_computation.1 | async-start | bytes 6455296 | tf_op jit(solution)/shard_map/all_to_all | solution.py:143
  131.2 188.5 %all-gather.7.cloned.1.call-start = ((), (), s32[]{:S(2)}) async-start(), calls=%async_computation.9 | async-start | bytes 4718592 | tf_op jit(solution)/shard_map/all_gather | solution.py:53
  204.2 75.8 %all-to-all-start = ((bf16[4,2,394,512]{3,1,2,0:T(2,128)(2,1)}), bf16[4,2,394,512]{3,1,2,0:T(2,128)(2,1)S(1)}, u32[]{:S(2)}, u32[]{:S(2)}) async-start(bf16[4,2,394,512]{3,1,2,0:T(2,128)(2,1)} %copy.153), calls=%async_computation | async-start | bytes 6455296 | tf_op jit(solution)/shard_map/all_to_all | solution.py:98
  208.0 144.6 %all-gather.9.cloned.1.call-start = ((), (), s32[]{:S(2)}) async-start(), calls=%async_computation.10 | async-start | bytes 4718592 | tf_op jit(solution)/shard_map/all_gather | solution.py:54
  317.9 56.5 %copy-start.39 = (bf16[1576,512]{1,0:T(8,128)(2,1)}, bf16[1576,512]{1,0:T(8,128)(2,1)S(1)}, u32[]{:S(2)}) copy-start(bf16[1576,512]{1,0:T(8,128)(2,1)S(1)} %squeeze.47) | copy-start | bytes 4841476
  319.7 32.9 %copy-start.35 = (bf16[1576,512]{1,0:T(8,128)(2,1)S(1)}, bf16[1576,512]{1,0:T(8,128)(2,1)}, u32[]{:S(2)}) copy-start(bf16[1576,512]{1,0:T(8,128)(2,1)} %squeeze.50) | copy-start | bytes 4841476
  352.6 15.5 %copy-start.74 = (bf16[2,512,2048]{2,1,0:T(8,128)(2,1)S(1)}, bf16[2,512,2048]{2,1,0:T(8,128)(2,1)}, u32[]{:S(2)}) copy-start(bf16[2,512,2048]{2,1,0:T(8,128)(2,1)} %all-gather.7.cloned.1.call-done) | copy-start | bytes 12582916
  374.5 32.5 %copy-start.37 = (bf16[1576,512]{1,0:T(8,128)(2,1)S(1)}, bf16[1576,512]{1,0:T(8,128)(2,1)}, u32[]{:S(2)}) copy-start(bf16[1576,512]{1,0:T(8,128)(2,1)} %squeeze.51) | copy-start | bytes 4841476
  440.7 160.2 %all-to-all-start.2 = ((bf16[1,2,1576,512]{3,1,0,2:T(2,128)(2,1)}), bf16[1,2,1576,512]{3,1,0,2:T(2,128)(2,1)}, u32[]{:S(2)}, u32[]{:S(2)}) async-start(bf16[1,2,1576,512]{3,1,0,2:T(2,128)(2,1)} %copy.162), calls=%async_computation.2 | async-start | bytes 6455296 | tf_op jit(solution)/shard_map/all_to_all | solution.py:169
  445.4 264.7 %reduce-scatter.16.cloned.1.call-start = ((), (), s32[]{:S(2)}) async-start(), calls=%async_computation.15 | async-start | bytes 147456
  445.9 7.2 copy-start.75
  460.0 8.7 copy-start.15
  460.0 10.1 %copy-start.69 = (s32[1576]{0:T(1024)S(1)}, s32[1576]{0:T(1024)}, u32[]{:S(2)}) copy-start(s32[1576]{0:T(1024)} %copy-done.68) | copy-start | bytes 18916
  461.7 54.3 %collective-permute-start = (bf16[1,2,394,512]{3,1,2,0:T(2,128)(2,1)}, bf16[1,2,394,512]{3,1,2,0:T(2,128)(2,1)}, u32[]{:S(2)}, u32[]{:S(2)}) collective-permute-start(bf16[1,2,394,512]{3,1,2,0:T(2,128)(2,1)} %copy.154), channel_id=1, source_target_pairs={{0,8},{8,0},{16,24},{24,16},{1,9},{9,1},{17,25},{25,17},{2,10},{10... | collective-permute-start | bytes 2420744 | tf_op jit(solution)/shard_map/ppermute | solution.py:125
  465.3 105.0 %collective-permute-start.1 = (bf16[1,2,394,512]{3,1,2,0:T(2,128)(2,1)}, bf16[1,2,394,512]{3,1,2,0:T(2,128)(2,1)}, u32[]{:S(2)}, u32[]{:S(2)}) collective-permute-start(bf16[1,2,394,512]{3,1,2,0:T(2,128)(2,1)} %copy.156), channel_id=1, source_target_pairs={{0,16},{8,24},{16,0},{24,8},{1,17},{9,25},{17,1},{25,9},{2,18},{10... | collective-permute-start | bytes 2420744 | tf_op jit(solution)/shard_map/ppermute | solution.py:125
  468.6 103.9 %collective-permute-start.2 = (bf16[1,2,394,512]{3,1,2,0:T(2,128)(2,1)S(1)}, bf16[1,2,394,512]{3,1,2,0:T(2,128)(2,1)}, u32[]{:S(2)}, u32[]{:S(2)}) collective-permute-start(bf16[1,2,394,512]{3,1,2,0:T(2,128)(2,1)S(1)} %copy.158), channel_id=1, source_target_pairs={{0,24},{8,16},{16,8},{24,0},{1,25},{9,17},{17,9},{25,1},{2,26},{10... | collective-permute-start | bytes 2420744 | tf_op jit(solution)/shard_map/ppermute | solution.py:125
  583.1 5.1 copy-start.24
  583.1 5.1 copy-start.32
  588.2 11.6 %copy-start.47 = (s32[788,2]{0,1:T(2,128)S(1)}, s32[788,2]{0,1:T(2,128)}, u32[]{:S(2)}) copy-start(s32[788,2]{0,1:T(2,128)} %param.13) | copy-start | bytes 18916
  588.2 11.6 %copy-start.45 = (f32[788,8]{0,1:T(8,128)S(1)}, f32[788,8]{0,1:T(8,128)}, u32[]{:S(2)}) copy-start(f32[788,8]{0,1:T(8,128)} %copy-done.44) | copy-start | bytes 75652
  588.2 11.6 %copy-start.51 = (f32[788]{0:T(1024)S(1)}, f32[788]{0:T(1024)}, u32[]{:S(2)}) copy-start(f32[788]{0:T(1024)} %copy-done.50) | copy-start | bytes 9460
  588.2 11.6 %copy-start.57 = (f32[788]{0:T(1024)S(1)}, f32[788]{0:T(1024)}, u32[]{:S(2)}) copy-start(f32[788]{0:T(1024)} %copy-done.56) | copy-start | bytes 9460
  588.2 11.6 %copy-start.7 = (bf16[788,512]{1,0:T(8,128)(2,1)S(1)}, bf16[788,512]{1,0:T(8,128)(2,1)}, u32[]{:S(2)}) copy-start(bf16[788,512]{1,0:T(8,128)(2,1)} %copy-done.5) | copy-start | bytes 2420740
  600.9 154.1 %reduce-scatter.10.cloned.1.call-start = ((), (), s32[]{:S(2)}) async-start(), calls=%async_computation.12 | async-start | bytes 589824 | tf_op jit(solution)/shard_map/reduce_scatter | solution.py:244
  618.9 5.9 copy-start.2
  618.9 5.9 copy-start.49
  618.9 5.9 copy-start.53
  618.9 5.9 copy-start.55
  618.9 5.9 copy-start.67
  631.9 5.3 copy-start.13
  631.9 12.8 %slice-start = ((s8[6553600]{0:T(1024)(128)(4,1)}), s8[4194304]{0:T(1024)(128)(4,1)S(1)}, s32[]{:S(2)}) async-start(s8[6553600]{0:T(1024)(128)(4,1)} %bitcast.152), calls=%async_computation.17 | async-start | bytes 8388608
  637.2 7.5 slice-start.1
  644.6 4.6 copy-start.11
  653.1 101.9 %reduce-scatter.8.cloned.1.call-start = ((), (), s32[]{:S(2)}) async-start(), calls=%async_computation.11 | async-start | bytes 1769472 | tf_op jit(solution)/shard_map/reduce_scatter | solution.py:241
  660.5 7.2 copy-start.4
  660.6 7.2 copy-start.59
  660.6 7.2 copy-start.65
  660.6 7.2 copy-start.71
  660.6 7.2 copy-start.73
  673.0 7.7 copy-start.40
  673.0 121.9 %reduce-scatter.12.cloned.1.call-start = ((), (), s32[]{:S(2)}) async-start(), calls=%async_computation.13 | async-start | bytes 4718592 | tf_op jit(solution)/shard_map/reduce_scatter | solution.py:179
  690.2 159.3 %reduce-scatter.14.cloned.1.call-start = ((), (), s32[]{:S(2)}) async-start(), calls=%async_computation.14 | async-start | bytes 4718592 | tf_op jit(solution)/shard_map/reduce_scatter | solution.py:182
  691.6 7.8 copy-start.38
  709.2 178.3 %all-reduce.17.cloned.1.call-start = ((), (), s32[]{:S(2)}) async-start(), calls=%async_computation.16 | async-start | bytes 524288 | tf_op jit(solution)/shard_map/psum | solution.py:260
  710.9 3.9 copy-start.61
  714.7 40.3 %copy-start.18 = (bf16[788,512]{1,0:T(8,128)(2,1)S(1)}, bf16[788,512]{1,0:T(8,128)(2,1)}, u32[]{:S(2)}) copy-start(bf16[788,512]{1,0:T(8,128)(2,1)} %param.14) | copy-start | bytes 2420740
  714.7 40.3 %copy-start.23 = (f32[788,512]{1,0:T(8,128)S(1)}, f32[788,512]{1,0:T(8,128)}, u32[]{:S(2)}) copy-start(f32[788,512]{1,0:T(8,128)} %copy-done.21) | copy-start | bytes 4841476
  (30 other events, 56.0 us)
Sparse Core Ops, SparseCore 0:
  10.5 28.3 all-gather.4
  134.4 37.0 all-gather.6
  210.7 37.0 all-gather.8
  601.0 44.9 reduce-scatter.15
  653.3 45.4 reduce-scatter.9
  701.9 38.4 reduce-scatter.7
  743.8 51.0 reduce-scatter.11
  798.3 51.0 reduce-scatter.13
  851.8 35.6 all-reduce.16
